TPU v7x, 128 devices: a whole 4x4x4 slice. The times are simulated.
128 devices in a mesh: row: 4 (over x_hi, core), col: 32 (over y, x_lo, z).
Axes of the slice: x: 4 (x_hi: 2, x_lo: 2; x = x_hi * 2 + x_lo), y: 4, z: 4, core: 2. Of those that a mesh axis runs over, the one named last changes fastest.
Arguments:
- tokens: bfloat16 [49152, 2048], P('col', 'row'), may hold values from -6 to 6
- in_weight: float32 [2048, 6144], P(('row', 'col')), may hold values from -0.125 to 0.125
- out_weight: float32 [2048, 2048], P(('row', 'col')), may hold values from -0.125 to 0.125
- beta_weight: float32 [2048, 16], replicated, may hold values from -0.25 to 0.25
- conv_weight: float32 [4, 6144], P(None, 'row'), may hold values from -2.5 to 2.5
- conv_prior: bfloat16 [96, 3, 6144], P('col', None, 'row'), may hold values from -6 to 6
- head_gain: float32 [2048], P('row'), may hold values from 0.1 to 1.9
- state_pool: float32 [192, 16, 128, 128], P('col', 'row'), may hold values from -2.5 to 2.5
- state_index: int32 [96, 16], P('col', 'row'), may hold values from 0 to 5
- lengths: int32 [96], P('col'), may hold values from 1 to 512, 36864 in all
- page_table: int32 [96, 4, 2], P('col'), may hold values from 0 to 31, as said below
Outputs:
- server_in: bfloat16 [2048, 6144], P('row', 'col')
- server_out: bfloat16 [2048, 2048], P('row', 'col')
- layer_out: bfloat16 [49152, 2048], P('col', 'row')
- final_state: float32 [96, 16, 128, 128], P('col', 'row')
- page_cache: bfloat16 [384, 128, 2, 2048], P('col', None, None, 'row')
Inputs may be any that keep to these rules, and one draw needn't show every extreme that they name: `lengths`: one prompt has all 512 tokens live. `state_index`: which of its own index of col's 6 stored states a prompt and head continues. page_table[p, g, 0] is the index of col that keeps page g of prompt p and page_table[p, g, 1] its slot there, below 12; every slot of every index of col gets exactly one page; the prompts of one index of col send at most 1 pages to any one index of col, and exactly 1 to some.
All inputs are finite; a program needn't handle non-finite values. No bound on the sum of `lengths` on one device may be relied on, other than what follows from the above.
Results may differ from a plain program's by a relative error of at most 0.029.
Values may be sent and summed in bfloat16 or wider, within the bound.
No kernel may reach another device: no remote copies, remote signals or barrier semaphores. Data moves between devices by JAX's collectives and lax.ppermute only.
A program may use at most 128 MiB of HBM per device.

v0:
```python
import jax
import jax.numpy as jnp
from jax import lax
from jax.sharding import PartitionSpec as P

DK = 128
STRETCH = 64
CONV = 4
SEQ = 512
PAGE = 128
PAGES_SEQ = 4
HIGHEST = lax.Precision.HIGHEST


def delta_block(carry_state, block_data):
    query_unit, key_unit, values, beta_rates = block_data
    width_c = beta_rates.shape[1]
    width_k = key_unit.shape[2]
    strict_lower = jnp.tril(jnp.ones((width_c, width_c), jnp.float32), -1)
    causal = jnp.tril(jnp.ones((width_c, width_c), jnp.float32))
    gram_matrix = jnp.einsum("bik,bjk->bij", key_unit, key_unit, precision=HIGHEST)
    system = (
        jnp.eye(width_c, dtype=jnp.float32) + beta_rates[:, :, None] * gram_matrix * strict_lower
    )
    right_side = jnp.concatenate([key_unit, values], axis=2) * beta_rates[:, :, None]
    solved = jax.scipy.linalg.solve_triangular(system, right_side, lower=True, unit_diagonal=True)
    weighted = solved[:, :, :width_k]
    corrected = solved[:, :, width_k:] - jnp.einsum(
        "bck,bkv->bcv", weighted, carry_state, precision=HIGHEST
    )
    scores = jnp.einsum("bik,bjk->bij", query_unit, key_unit, precision=HIGHEST) * causal
    output = jnp.einsum("bck,bkv->bcv", query_unit, carry_state, precision=HIGHEST) + jnp.einsum(
        "bij,bjv->biv", scores, corrected, precision=HIGHEST
    )
    carry_state = carry_state + jnp.einsum("bck,bcv->bkv", key_unit, corrected, precision=HIGHEST)
    return (carry_state, output)


def delta_scan(query_unit, key_unit, values, beta_rates, initial, block_len):
    batch_n = query_unit.shape[0]
    length_all = query_unit.shape[1]
    num_blocks = length_all // block_len

    def to_blocks(tensor):
        shaped = tensor.reshape((batch_n, num_blocks, block_len) + tensor.shape[2:])
        return jnp.moveaxis(shaped, 1, 0)

    last_state, outputs = lax.scan(
        delta_block,
        initial,
        (to_blocks(query_unit), to_blocks(key_unit), to_blocks(values), to_blocks(beta_rates)),
    )
    outputs = jnp.moveaxis(outputs, 0, 1).reshape(batch_n, length_all, -1)
    return (last_state, outputs)


def unit_rows(tensor):
    return tensor * lax.rsqrt(jnp.sum(tensor * tensor, axis=-1, keepdims=True) + 1e-06)


def local(
    tokens,
    in_weight,
    out_weight,
    beta_weight,
    conv_weight,
    conv_prior,
    head_gain,
    state_pool,
    state_index,
    lengths,
    page_table,
):
    row_count = lax.axis_size("row")
    col_count = lax.axis_size("col")
    row_id = lax.axis_index("row")
    local_tokens = tokens.shape[0]
    feature_span = tokens.shape[1]
    head_group = state_index.shape[1]
    head_width = 3 * DK
    prompts_here = lengths.shape[0]
    trainer_in = in_weight.astype(jnp.bfloat16)
    server_in, server_out = (
        lax.all_to_all(trainer_in, "col", split_axis=1, concat_axis=0, tiled=True),
        lax.all_to_all(
            out_weight.astype(jnp.bfloat16), "col", split_axis=1, concat_axis=0, tiled=True
        ),
    )
    beta_cast = beta_weight.astype(jnp.bfloat16)
    wide_in, wide_out = (
        lax.all_gather(server_in, "col", axis=1, tiled=True),
        lax.all_gather(server_out, "col", axis=1, tiled=True),
    )
    columns = wide_in
    product = jnp.dot(tokens, columns, preferred_element_type=jnp.float32)
    qkv_sum = lax.psum_scatter(
        product.reshape(local_tokens, lax.axis_size("row") * head_group, head_width)
        .transpose(1, 0, 2)
        .astype(jnp.bfloat16),
        "row",
        scatter_dimension=0,
        tiled=True,
    )
    beta_rows = lax.dynamic_slice_in_dim(beta_cast, row_id * feature_span, feature_span, 0)
    beta_term = jnp.dot(tokens, beta_rows, preferred_element_type=jnp.float32).T
    beta_sum = lax.psum_scatter(
        beta_term.astype(jnp.bfloat16), "row", scatter_dimension=0, tiled=True
    ).astype(jnp.float32)
    projected = qkv_sum.reshape(head_group, prompts_here, SEQ, head_width)
    prior_rows = conv_prior.reshape(prompts_here, CONV - 1, head_group, head_width).transpose(
        2, 0, 1, 3
    )
    padded = jnp.concatenate(
        [prior_rows.astype(jnp.float32), projected.astype(jnp.float32)], axis=2
    )
    taps_all = conv_weight.reshape(CONV, head_group, head_width)
    conv_sum = jnp.zeros(projected.shape, jnp.float32)
    for tap_id in range(CONV):
        conv_sum = (
            conv_sum + taps_all[tap_id][:, None, None, :] * padded[:, :, tap_id : tap_id + SEQ]
        )
    activated = jax.nn.silu(conv_sum).reshape(head_group * prompts_here, SEQ, 3, DK)
    query_unit = unit_rows(activated[:, :, 0])
    key_unit = unit_rows(activated[:, :, 1])
    values = activated[:, :, 2]
    live_mask = (jnp.arange(SEQ, dtype=jnp.int32)[None, :] < lengths[:, None]).astype(jnp.float32)
    live_batch = jnp.broadcast_to(live_mask[None], (head_group, prompts_here, SEQ)).reshape(
        head_group * prompts_here, SEQ
    )
    beta_rates = live_batch * jax.nn.sigmoid(beta_sum.reshape(head_group * prompts_here, SEQ))
    picked = state_pool[state_index, jnp.arange(head_group, dtype=jnp.int32)[None, :]]
    initial = picked.transpose(1, 0, 2, 3).reshape(head_group * prompts_here, DK, DK)
    last_state, outputs = delta_scan(query_unit, key_unit, values, beta_rates, initial, STRETCH)
    outputs = outputs * live_batch[:, :, None]
    normed = outputs.reshape(head_group, prompts_here, SEQ, DK)
    normed = (
        normed
        * lax.rsqrt(jnp.mean(normed * normed, axis=3, keepdims=True) + 1e-05)
        * head_gain.reshape(head_group, 1, 1, DK)
    )
    flat_heads = (
        normed.astype(jnp.bfloat16).transpose(1, 2, 0, 3).reshape(local_tokens, head_group * DK)
    )
    out_span = wide_out.shape[1] // row_count
    columns = wide_out
    product = jnp.dot(flat_heads, columns, preferred_element_type=jnp.float32)
    layer_out = (
        lax.psum_scatter(
            product.reshape(local_tokens, lax.axis_size("row") * 1, out_span)
            .transpose(1, 0, 2)
            .astype(jnp.bfloat16),
            "row",
            scatter_dimension=0,
            tiled=True,
        )
        .astype(jnp.float32)[0]
        .astype(jnp.bfloat16)
    )
    final_state = last_state.reshape(head_group, prompts_here, DK, DK).transpose(1, 0, 2, 3)
    keep_mask = live_batch[:, :, None]
    kept_pairs = jnp.stack([key_unit * keep_mask, values * keep_mask], axis=0).reshape(
        2, head_group, prompts_here, SEQ, DK
    )
    page_rows = (
        kept_pairs.transpose(2, 3, 0, 1, 4)
        .reshape(prompts_here * PAGES_SEQ, PAGE, 2, head_group * DK)
        .astype(jnp.bfloat16)
    )
    pages_dev = page_rows.shape[0]
    capacity = max(1, 2 * pages_dev // col_count)
    targets = page_table[:, :, 0].reshape(-1)
    slot_ids = page_table[:, :, 1].reshape(-1)
    order_ids = jnp.arange(pages_dev, dtype=jnp.int32)
    earlier = (targets[:, None] == targets[None, :]) & (order_ids[None, :] < order_ids[:, None])
    positions = targets * capacity + jnp.sum(earlier.astype(jnp.int32), axis=1)
    outgoing = (
        jnp.zeros((col_count * capacity,) + page_rows.shape[1:], jnp.bfloat16)
        .at[positions]
        .set(page_rows)
    )
    slot_send = jnp.full((col_count * capacity,), pages_dev, jnp.int32).at[positions].set(slot_ids)
    arrived, arrived_slots = (
        lax.all_to_all(outgoing, "col", split_axis=0, concat_axis=0, tiled=True),
        lax.all_to_all(slot_send, "col", split_axis=0, concat_axis=0, tiled=True),
    )
    page_cache = (
        jnp.zeros(page_rows.shape, jnp.bfloat16).at[arrived_slots].set(arrived, mode="drop")
    )
    return (server_in, server_out, layer_out, final_state, page_cache)


def solution(mesh):
    return jax.shard_map(
        local,
        mesh=mesh,
        in_specs=(
            P("col", "row"),
            P(("row", "col"), None),
            P(("row", "col"), None),
            P(),
            P(None, "row"),
            P("col", None, "row"),
            P("row"),
            P("col", "row", None, None),
            P("col", "row"),
            P("col"),
            P("col", None, None),
        ),
        out_specs=(
            P("row", "col"),
            P("row", "col"),
            P("col", "row"),
            P("col", "row", None, None),
            P("col", None, None, "row"),
        ),
        check_vma=False,
    )
```

profile of v0, /device:TPU:16, one launch (start us, length us, event | category | flops | bytes accessed | tf_op | source)
XLA Modules:
  0.0 1226.2 jit_solution(3627169898886624098)
XLA Ops:
  8.8 16.4 %all_to_all.55 = bf16[16,32,192]{2,0,1:T(8,128)(2,1)S(1)} all-to-all(bf16[16,32,192]{2,0,1:T(8,128)(2,1)S(1)} %copy.123), channel_id=1, replica_groups=mesh['row'=4,'col'=32] {'col'}, dimensions={1} | all-to-all | bytes 393216 | tf_op jit(solution)/shard_map/all_to_all | solution.py:84
  26.1 144.7 %all-gather.3.cloned.1.call-done = bf16[512,6144]{0,1:T(8,128)(2,1)} async-done(((bf16[512,192]{0,1:T(8,128)(2,1)}), bf16[512,6144]{0,1:T(8,128)(2,1)}) %all-gather.3.cloned.1.call-update) | async-done | bytes 6291472 | tf_op jit(solution)/shard_map/all_gather | solution.py:91
  170.8 15.9 %convolution_convert_fusion = bf16[1536,6144]{1,0:T(8,128)(2,1)} fusion(bf16[1536,512]{1,0:T(8,128)(2,1)S(1)} %copy-done, bf16[512,6144]{0,1:T(8,128)(2,1)} %all-gather.3.cloned.1.call-done), kind=kOutput, calls=%fused_computation.43 | convolution fusion | flops 9673113600 | bytes 26738688 | tf_op jit(solution)/shard_map/dot_general | solution.py:95
  186.7 18.3 %copy.164 = bf16[192,16,8,384]{3,2,0,1:T(8,128)(2,1)} copy(bf16[192,16,8,384]{3,2,1,0:T(8,128)(2,1)} %bitcast.161) | data formatting | bytes 37748736 | tf_op jit(solution)/shard_map/convert_element_type | solution.py:99
  207.0 25.2 %all-to-all-start.1 = ((bf16[32,2,512]{2,1,0:T(2,128)(2,1)}), bf16[32,2,512]{2,1,0:T(2,128)(2,1)S(1)}, u32[]{:S(2)}, u32[]{:S(2)}) async-start(bf16[32,2,512]{2,1,0:T(2,128)(2,1)} %reshape.338), calls=%async_computation.1 | async-start | bytes 131072 | tf_op jit(solution)/shard_map/all_to_all | solution.py:85
  234.8 13.6 %all-reduce = bf16[16,1536]{1,0:T(8,128)(2,1)S(1)} all-reduce(bf16[16,1536]{1,0:T(8,128)(2,1)S(1)} %convolution_convert_fusion.1), channel_id=3, replica_groups=mesh['row'=4,'col'=32] {'row'}, use_global_device_ids=true, to_apply=%region_3.4.clone | all-reduce | flops 24576 | bytes 98304
  252.5 116.9 %reduce-scatter.3.cloned.1.call-done = bf16[4,1536,384]{2,1,0:T(8,128)(2,1)} async-done(((bf16[16,1536,384]{2,1,0:T(8,128)(2,1)}), bf16[4,1536,384]{2,1,0:T(8,128)(2,1)}) %reduce-scatter.3.cloned.1.call-update) | async-done | bytes 4718608 | tf_op jit(solution)/shard_map/reduce_scatter | solution.py:96
  372.6 7.4 divide_multiply_fusion
  380.0 9.7 copy.129
  389.6 8.1 multiply_reduce_fusion
  414.5 554.7 %while.12 = (s32[]{:T(128)}, f32[12,128,128]{2,1,0:T(8,128)S(1)}, f32[8,12,64,128]{3,2,0,1:T(8,128)}, f32[8,12,64,128]{3,2,0,1:T(8,128)}, f32[8,12,64]{2,0,1:T(8...) while((s32[]{:T(128)}, f32[12,128,128]{2,1,0:T(8,128)S(1)}, ...), condition=%wide.region_5.6_spmd, body=%wide.region_4.5_spmd.sunk | while | flops 831590464 | bytes 12349789 | solution.py:48
  416.7 59.0 %custom-call.8 = f32[12,1,64,64]{2,3,1,0:T(8,128)S(1)} custom-call(f32[12,1,64,64]{3,2,1,0:T(8,128)S(1)} %fusion.93), custom_call_target="InvertDiagBlocksLowerTriangular" | custom-call | tf_op jit(solution)/shard_map/while/body/eval_jaxpr/jit(_solve_triangular)/vmap()/triangular_solve | solution.py:26
  486.0 59.0 %custom-call.8 = f32[12,1,64,64]{2,3,1,0:T(8,128)S(1)} custom-call(f32[12,1,64,64]{3,2,1,0:T(8,128)S(1)} %fusion.93), custom_call_target="InvertDiagBlocksLowerTriangular" | custom-call | tf_op jit(solution)/shard_map/while/body/eval_jaxpr/jit(_solve_triangular)/vmap()/triangular_solve | solution.py:26
  555.4 59.0 %custom-call.8 = f32[12,1,64,64]{2,3,1,0:T(8,128)S(1)} custom-call(f32[12,1,64,64]{3,2,1,0:T(8,128)S(1)} %fusion.93), custom_call_target="InvertDiagBlocksLowerTriangular" | custom-call | tf_op jit(solution)/shard_map/while/body/eval_jaxpr/jit(_solve_triangular)/vmap()/triangular_solve | solution.py:26
  624.7 59.0 %custom-call.8 = f32[12,1,64,64]{2,3,1,0:T(8,128)S(1)} custom-call(f32[12,1,64,64]{3,2,1,0:T(8,128)S(1)} %fusion.93), custom_call_target="InvertDiagBlocksLowerTriangular" | custom-call | tf_op jit(solution)/shard_map/while/body/eval_jaxpr/jit(_solve_triangular)/vmap()/triangular_solve | solution.py:26
  694.0 59.0 %custom-call.8 = f32[12,1,64,64]{2,3,1,0:T(8,128)S(1)} custom-call(f32[12,1,64,64]{3,2,1,0:T(8,128)S(1)} %fusion.93), custom_call_target="InvertDiagBlocksLowerTriangular" | custom-call | tf_op jit(solution)/shard_map/while/body/eval_jaxpr/jit(_solve_triangular)/vmap()/triangular_solve | solution.py:26
  763.4 59.0 %custom-call.8 = f32[12,1,64,64]{2,3,1,0:T(8,128)S(1)} custom-call(f32[12,1,64,64]{3,2,1,0:T(8,128)S(1)} %fusion.93), custom_call_target="InvertDiagBlocksLowerTriangular" | custom-call | tf_op jit(solution)/shard_map/while/body/eval_jaxpr/jit(_solve_triangular)/vmap()/triangular_solve | solution.py:26
  832.7 59.0 %custom-call.8 = f32[12,1,64,64]{2,3,1,0:T(8,128)S(1)} custom-call(f32[12,1,64,64]{3,2,1,0:T(8,128)S(1)} %fusion.93), custom_call_target="InvertDiagBlocksLowerTriangular" | custom-call | tf_op jit(solution)/shard_map/while/body/eval_jaxpr/jit(_solve_triangular)/vmap()/triangular_solve | solution.py:26
  902.0 59.0 %custom-call.8 = f32[12,1,64,64]{2,3,1,0:T(8,128)S(1)} custom-call(f32[12,1,64,64]{3,2,1,0:T(8,128)S(1)} %fusion.93), custom_call_target="InvertDiagBlocksLowerTriangular" | custom-call | tf_op jit(solution)/shard_map/while/body/eval_jaxpr/jit(_solve_triangular)/vmap()/triangular_solve | solution.py:26
  978.6 8.2 convert_bitcast_fusion
  989.3 7.6 all-to-all-start.2
  997.2 5.3 copy.142
  1002.5 4.9 copy.143
  1007.4 9.9 multiply_convert_fusion.1
  1017.4 3.9 maximum_bitcast_fusion
  1021.3 5.7 reshape.308
  1030.9 4.2 broadcast_in_dim.32
  1035.1 8.4 scatter_fusion
  1043.5 8.3 all-to-all-start.3
  1053.5 139.6 %all-to-all-done.3 = bf16[32,128,2,512]{3,1,2,0:T(8,128)(2,1)} async-done(((bf16[32,128,2,512]{3,1,2,0:T(8,128)(2,1)}), bf16[32,128,2,512]{3,1,2,0:T(8,128)(2,1)}, u32[]{:S(2)}, u32[]{:S(2)}) %all-to-all-start.3) | async-done | bytes 8388640 | tf_op jit(solution)/shard_map/all_to_all | solution.py:183
  1195.2 17.7 %scatter_fusion.1 = bf16[12,128,2,512]{3,1,2,0:T(8,128)(2,1)} fusion(bf16[12,128,2,512]{3,1,2,0:T(8,128)(2,1)} %broadcast_in_dim.25, s32[32]{0:T(128)S(1)} %fusion.41, bf16[32,128,2,512]{3,1,2,0:T(8,128)(2,1)} %all-to-all-done.3), kind=kCustom, calls=%fused_computation.3 | custom fusion | bytes 25165952 | tf_op jit(solution)/shard_map/scatter | solution.py:187
  1212.8 6.8 copy.148
  (214 shorter events, 131.9 us)
Async XLA Ops:
  7.2 163.6 %copy-start = (bf16[1536,512]{1,0:T(8,128)(2,1)S(1)}, bf16[1536,512]{1,0:T(8,128)(2,1)}, u32[]{:S(2)}) copy-start(bf16[1536,512]{1,0:T(8,128)(2,1)} %param.13) | copy-start | bytes 4718596
  7.2 163.6 %all-gather.3.cloned.1.call-start = ((), (), s32[]{:S(2)}) async-start(), calls=%async_computation.6 | async-start | bytes 6488064 | tf_op jit(solution)/shard_map/all_gather | solution.py:91
  26.1 343.3 %reduce-scatter.3.cloned.1.call-start = ((), (), s32[]{:S(2)}) async-start(), calls=%async_computation.7 | async-start | bytes 23592960 | tf_op jit(solution)/shard_map/reduce_scatter | solution.py:96
  205.0 0.9 copy-start.3
  205.0 27.3 %copy-start.10 = (u32[128]{0:T(128)S(1)}, u32[128]{0:T(128)}, u32[]{:S(2)}) copy-start(u32[128]{0:T(128)} %constant.92) | copy-start | bytes 1540
  205.0 43.5 %copy-start.9 = (s32[3]{0:T(128)S(1)}, s32[3]{0:T(128)}, u32[]{:S(2)}) copy-start(s32[3]{0:T(128)} %param.22) | copy-start | bytes 40
  205.0 43.7 %copy-start.8 = (s32[3,4]{1,0:T(4,128)S(1)}, s32[3,4]{1,0:T(4,128)}, u32[]{:S(2)}) copy-start(s32[3,4]{1,0:T(4,128)} %param.21) | copy-start | bytes 148
  205.9 42.9 %copy-start.5 = (f32[4,1536]{1,0:T(4,128)S(1)}, f32[4,1536]{1,0:T(4,128)}, u32[]{:S(2)}) copy-start(f32[4,1536]{1,0:T(4,128)} %param.17) | copy-start | bytes 73732
  205.9 43.0 %copy-start.4 = (bf16[3,3,1536]{2,1,0:T(4,128)(2,1)S(1)}, bf16[3,3,1536]{2,1,0:T(4,128)(2,1)}, u32[]{:S(2)}) copy-start(bf16[3,3,1536]{2,1,0:T(4,128)(2,1)} %param.18) | copy-start | bytes 82948
  207.0 44.6 %all-to-all-start.1 = ((bf16[32,2,512]{2,1,0:T(2,128)(2,1)}), bf16[32,2,512]{2,1,0:T(2,128)(2,1)S(1)}, u32[]{:S(2)}, u32[]{:S(2)}) async-start(bf16[32,2,512]{2,1,0:T(2,128)(2,1)} %reshape.338), calls=%async_computation.1 | async-start | bytes 131072 | tf_op jit(solution)/shard_map/all_to_all | solution.py:85
  232.2 746.4 %all-gather.5.cloned.1.call-start = ((), (), s32[]{:S(2)}) async-start(), calls=%async_computation.8 | async-start | bytes 2162688 | tf_op jit(solution)/shard_map/all_gather | solution.py:92
  252.4 967.2 %reduce-scatter.5.cloned.1.call-start = ((), (), s32[]{:S(2)}) async-start(), calls=%async_computation.9 | async-start | bytes 7864320 | tf_op jit(solution)/shard_map/reduce_scatter | solution.py:148
  408.6 3.8 copy-start.2
  969.2 3.6 copy-start.7
  986.8 0.7 copy-start.6
  989.3 54.2 %all-to-all-start.2 = ((s32[32,1,1]{2,1,0:T(1,128)}), s32[32,1,1]{2,1,0:T(1,128)S(1)}, u32[]{:S(2)}, u32[]{:S(2)}) async-start(s32[32,1,1]{2,1,0:T(1,128)} %copy.140), calls=%async_computation.4 | async-start | bytes 32768 | tf_op jit(solution)/shard_map/all_to_all | solution.py:184
  1043.5 149.6 %all-to-all-start.3 = ((bf16[32,128,2,512]{3,1,2,0:T(8,128)(2,1)}), bf16[32,128,2,512]{3,1,2,0:T(8,128)(2,1)}, u32[]{:S(2)}, u32[]{:S(2)}) async-start(bf16[32,128,2,512]{3,1,2,0:T(8,128)(2,1)} %scatter_fusion), calls=%async_computation.5 | async-start | bytes 16777216 | tf_op jit(solution)/shard_map/all_to_all | solution.py:183
  1195.2 24.5 %copy-start.1 = (bf16[1536,512]{1,0:T(8,128)(2,1)S(1)}, bf16[1536,512]{1,0:T(8,128)(2,1)}, u32[]{:S(2)}) copy-start(bf16[1536,512]{1,0:T(8,128)(2,1)} %param.13) | copy-start | bytes 4718596
Sparse Core Ops, SparseCore 0:
  26.2 144.5 all-gather.2
  205.2 164.0 reduce-scatter.2
  371.7 135.9 all-gather.4
  987.0 64.7 reduce-scatter.4
where the time goes:
time: 1230 us
  other arithmetic  520 us (42%)
  waiting for transfers between devices  401 us (33%)
  local copies, waits for them, and re-layouts  122 us (10%)
  matrix products  96.3 us (8%)
  starting transfers between devices  41.4 us (3%)
  blocking collectives  30 us (2%)
  between operations  14.8 us (1%)
    another operation x32, other arithmetic, delta_block(): jax.scipy.linalg.solve_triangular(system, right_side, lower=True, unit_di...  473 us
    all_gather x1, waiting for transfers between devices, local(): lax.all_gather(server_in, 'col', axis=1, tiled=True)  145 us
    all_to_all x1, waiting for transfers between devices, local(): lax.all_to_all(outgoing, 'col', split_axis=0, concat_axis=0, tiled=True)  140 us
    reduce_scatter x1, waiting for transfers between devices, local(): lax.psum_scatter(product.reshape(local_tokens, lax.axis_size('row') * hea...  117 us
    all_to_all x1, starting transfers between devices, local(): lax.all_to_all(out_weight.astype(jnp.bfloat16), 'col', split_axis=1, conc...  25.2 us
  transfers between devices with their start and end apart: 7, of which 3 were waited for; matrix products, arithmetic and copies ran while one was open for 56% of the time, Pallas kernels for 0%

commit v1 on v0

--- a/solution.py
+++ b/solution.py
@@ -10,6 +10,16 @@
 PAGE = 128
 PAGES_SEQ = 4
 HIGHEST = lax.Precision.HIGHEST
+
+
+def answer_trails_here(arr):
+    w2 = lax.all_to_all(
+        jnp.stack(lax.axis_size("col") * [arr], axis=0),
+        axis_name="col",
+        split_axis=0,
+        concat_axis=0,
+    )
+    return jnp.concatenate(w2, axis=1)
 
 
 def delta_block(carry_state, block_data):
@@ -88,7 +98,7 @@
     )
     beta_cast = beta_weight.astype(jnp.bfloat16)
     wide_in, wide_out = (
-        lax.all_gather(server_in, "col", axis=1, tiled=True),
+        answer_trails_here(server_in),
         lax.all_gather(server_out, "col", axis=1, tiled=True),
     )
     columns = wide_in

time: 1230 us -> 1130 us (0.919)
  waiting for transfers between devices: 401 us -> 255 us
  blocking collectives: 30 us -> 107 us
  local copies, waits for them, and re-layouts: 122 us -> 103 us
  starting transfers between devices: 41.4 us -> 22.8 us
    all_gather x1 -> x0, waiting for transfers between devices: 145 us -> none  [local(): lax.all_gather(server_in, 'col', axis=1, tiled=True)]
    all_to_all x0 -> x1, blocking collectives: none -> 75.7 us  [answer_trails_here(): lax.all_to_all(jnp.stack(lax.axis_size('col') * [arr], axis=0), axis_name...]
    all_to_all x1, starting transfers between devices: 25.2 us -> 6.31 us  [local(): lax.all_to_all(out_weight.astype(jnp.bfloat16), 'col', split_axis=1, conc...]
  transfers between devices with their start and end apart: 7 -> 6, of which waited for: 3 -> 2; matrix products, arithmetic and copies ran while one was open for 56% -> 62% of each run, Pallas kernels for 0% -> 0%
where the time goes in v1:
time: 1130 us; the launch traced here: 1120 us
  other arithmetic  523 us (46%)
  waiting for transfers between devices  255 us (23%)
  blocking collectives  107 us (9%)
  local copies, waits for them, and re-layouts  103 us (9%)
  matrix products  96.3 us (9%)
  starting transfers between devices  22.8 us (2%)
  between operations  16.8 us (1%)
    another operation x32, other arithmetic, delta_block(): jax.scipy.linalg.solve_triangular(system, right_side, lower=True, unit_di...  473 us
    all_to_all x1, waiting for transfers between devices, local(): lax.all_to_all(outgoing, 'col', split_axis=0, concat_axis=0, tiled=True)  136 us
    reduce_scatter x1, waiting for transfers between devices, local(): lax.psum_scatter(product.reshape(local_tokens, lax.axis_size('row') * hea...  119 us
    all_to_all x1, blocking collectives, answer_trails_here(): lax.all_to_all(jnp.stack(lax.axis_size('col') * [arr], axis=0), axis_name...  75.7 us
  transfers between devices with their start and end apart: 6, of which 2 were waited for; matrix products, arithmetic and copies ran while one was open for 62% of the time, Pallas kernels for 0%

profile of v1, /device:TPU:16, one launch (start us, length us, event | category | flops | bytes accessed | tf_op | source)
XLA Modules:
  0.0 1124.4 jit_solution(16898260078840495810)
XLA Ops:
  9.7 16.4 %all_to_all.60 = bf16[16,32,192]{2,0,1:T(8,128)(2,1)S(1)} all-to-all(bf16[16,32,192]{2,0,1:T(8,128)(2,1)S(1)} %copy.128), channel_id=1, replica_groups=mesh['row'=4,'col'=32] {'col'}, dimensions={1} | all-to-all | bytes 393216 | tf_op jit(solution)/shard_map/all_to_all | solution.py:94
  26.9 75.7 %all_to_all.61 = bf16[32,512,192]{1,2,0:T(8,128)(2,1)} all-to-all(bf16[32,512,192]{1,2,0:T(8,128)(2,1)S(1)} %stack.4), channel_id=1, replica_groups=mesh['row'=4,'col'=32] {'col'}, dimensions={0} | all-to-all | bytes 12582912 | tf_op jit(solution)/shard_map/all_to_all | solution.py:16
  102.6 15.9 %convert_bitcast_fusion = bf16[16,1536,384]{2,1,0:T(8,128)(2,1)} fusion(bf16[16,384,512]{2,1,0:T(8,128)(2,1)} %bitcast.168, bf16[1536,512]{1,0:T(8,128)(2,1)S(1)} %copy-done), kind=kOutput, calls=%fused_computation.43 | convolution fusion | flops 9673113600 | bytes 26738688 | tf_op jit(solution)/shard_map/dot_general | solution.py:105
  120.4 6.3 all-to-all-start.1
  129.3 14.6 %all-reduce = bf16[16,1536]{1,0:T(8,128)(2,1)S(1)} all-reduce(bf16[16,1536]{1,0:T(8,128)(2,1)S(1)} %convolution_convert_fusion), channel_id=3, replica_groups=mesh['row'=4,'col'=32] {'row'}, use_global_device_ids=true, to_apply=%region_3.4.clone | all-reduce | flops 24576 | bytes 98304
  150.1 118.6 %reduce-scatter.3.cloned.1.call-done = bf16[4,1536,384]{2,1,0:T(8,128)(2,1)} async-done(((bf16[16,1536,384]{2,1,0:T(8,128)(2,1)}), bf16[4,1536,384]{2,1,0:T(8,128)(2,1)}) %reduce-scatter.3.cloned.1.call-update) | async-done | bytes 4718608 | tf_op jit(solution)/shard_map/reduce_scatter | solution.py:106
  268.8 7.5 copy.133
  276.3 17.4 %divide_multiply_fusion = f32[4,3,512,384]{2,3,1,0:T(8,128)S(1)} fusion(f32[4,3,512,384]{2,3,1,0:T(8,128)} %copy.133, f32[4,3,3,384]{2,3,1,0:T(8,128)} %copy.132, f32[4,384]{1,0:T(4,128)S(1)} %mul.198, f32[4,384]{1,0:T(4,128)S(1)} %mul.195, f32[4,384]{1,0:T(4,128)S(1)} %mul.192, f32[4,384]{1,0:T(4,128)S(1)} %mul.189), kind=kLoop, calls=%fused_computation.57 | loop fusion | flops 33030144 | bytes 18954240 | tf_op jit(solution)/shard_map/jit(silu)/mul | solution.py:132
  293.7 4.1 multiply_reduce_fusion
  314.5 555.2 %while.12 = (s32[]{:T(128)}, f32[12,128,128]{2,1,0:T(8,128)S(1)}, f32[8,12,64,128]{3,2,0,1:T(8,128)}, f32[8,12,64,128]{3,2,0,1:T(8,128)}, f32[8,12,64]{2,0,1:T(8...) while((s32[]{:T(128)}, f32[12,128,128]{2,1,0:T(8,128)S(1)}, ...), condition=%wide.region_5.6_spmd, body=%wide.region_4.5_spmd.sunk | while | flops 831590464 | bytes 12349789 | solution.py:58
  317.2 59.0 %custom-call.8 = f32[12,1,64,64]{2,3,1,0:T(8,128)S(1)} custom-call(f32[12,1,64,64]{3,2,1,0:T(8,128)S(1)} %fusion.93), custom_call_target="InvertDiagBlocksLowerTriangular" | custom-call | tf_op jit(solution)/shard_map/while/body/eval_jaxpr/jit(_solve_triangular)/vmap()/triangular_solve | solution.py:36
  386.5 59.0 %custom-call.8 = f32[12,1,64,64]{2,3,1,0:T(8,128)S(1)} custom-call(f32[12,1,64,64]{3,2,1,0:T(8,128)S(1)} %fusion.93), custom_call_target="InvertDiagBlocksLowerTriangular" | custom-call | tf_op jit(solution)/shard_map/while/body/eval_jaxpr/jit(_solve_triangular)/vmap()/triangular_solve | solution.py:36
  455.9 59.0 %custom-call.8 = f32[12,1,64,64]{2,3,1,0:T(8,128)S(1)} custom-call(f32[12,1,64,64]{3,2,1,0:T(8,128)S(1)} %fusion.93), custom_call_target="InvertDiagBlocksLowerTriangular" | custom-call | tf_op jit(solution)/shard_map/while/body/eval_jaxpr/jit(_solve_triangular)/vmap()/triangular_solve | solution.py:36
  525.2 59.0 %custom-call.8 = f32[12,1,64,64]{2,3,1,0:T(8,128)S(1)} custom-call(f32[12,1,64,64]{3,2,1,0:T(8,128)S(1)} %fusion.93), custom_call_target="InvertDiagBlocksLowerTriangular" | custom-call | tf_op jit(solution)/shard_map/while/body/eval_jaxpr/jit(_solve_triangular)/vmap()/triangular_solve | solution.py:36
  594.5 59.0 %custom-call.8 = f32[12,1,64,64]{2,3,1,0:T(8,128)S(1)} custom-call(f32[12,1,64,64]{3,2,1,0:T(8,128)S(1)} %fusion.93), custom_call_target="InvertDiagBlocksLowerTriangular" | custom-call | tf_op jit(solution)/shard_map/while/body/eval_jaxpr/jit(_solve_triangular)/vmap()/triangular_solve | solution.py:36
  663.9 59.0 %custom-call.8 = f32[12,1,64,64]{2,3,1,0:T(8,128)S(1)} custom-call(f32[12,1,64,64]{3,2,1,0:T(8,128)S(1)} %fusion.93), custom_call_target="InvertDiagBlocksLowerTriangular" | custom-call | tf_op jit(solution)/shard_map/while/body/eval_jaxpr/jit(_solve_triangular)/vmap()/triangular_solve | solution.py:36
  733.2 59.0 %custom-call.8 = f32[12,1,64,64]{2,3,1,0:T(8,128)S(1)} custom-call(f32[12,1,64,64]{3,2,1,0:T(8,128)S(1)} %fusion.93), custom_call_target="InvertDiagBlocksLowerTriangular" | custom-call | tf_op jit(solution)/shard_map/while/body/eval_jaxpr/jit(_solve_triangular)/vmap()/triangular_solve | solution.py:36
  802.5 59.0 %custom-call.8 = f32[12,1,64,64]{2,3,1,0:T(8,128)S(1)} custom-call(f32[12,1,64,64]{3,2,1,0:T(8,128)S(1)} %fusion.93), custom_call_target="InvertDiagBlocksLowerTriangular" | custom-call | tf_op jit(solution)/shard_map/while/body/eval_jaxpr/jit(_solve_triangular)/vmap()/triangular_solve | solution.py:36
  879.1 8.2 convert_bitcast_fusion.1
  889.8 7.4 all-to-all-start.3
  897.5 5.2 copy.147
  902.7 5.0 copy.148
  907.6 9.9 multiply_convert_fusion.1
  917.6 3.9 maximum_bitcast_fusion
  921.5 5.7 reshape.319
  927.3 3.9 copy.149
  931.1 4.2 broadcast_in_dim.32
  935.4 8.4 scatter_fusion
  943.7 8.7 all-to-all-start.4
  954.1 136.0 %all-to-all-done.4 = bf16[32,128,2,512]{3,1,2,0:T(8,128)(2,1)} async-done(((bf16[32,128,2,512]{3,1,2,0:T(8,128)(2,1)}), bf16[32,128,2,512]{3,1,2,0:T(8,128)(2,1)}, u32[]{:S(2)}, u32[]{:S(2)}) %all-to-all-start.4) | async-done | bytes 8388640 | tf_op jit(solution)/shard_map/all_to_all | solution.py:193
  1092.2 17.7 %scatter_fusion.1 = bf16[12,128,2,512]{3,1,2,0:T(8,128)(2,1)} fusion(bf16[12,128,2,512]{3,1,2,0:T(8,128)(2,1)} %broadcast_in_dim.25, s32[32]{0:T(128)S(1)} %fusion.42, bf16[32,128,2,512]{3,1,2,0:T(8,128)(2,1)} %all-to-all-done.4), kind=kCustom, calls=%fused_computation.3 | custom fusion | bytes 25165952 | tf_op jit(solution)/shard_map/scatter | solution.py:197
  1109.9 6.8 copy.153
  (213 shorter events, 126.8 us)
Async XLA Ops:
  8.0 94.6 %copy-start = (bf16[1536,512]{1,0:T(8,128)(2,1)S(1)}, bf16[1536,512]{1,0:T(8,128)(2,1)}, u32[]{:S(2)}) copy-start(bf16[1536,512]{1,0:T(8,128)(2,1)} %param.13) | copy-start | bytes 4718596
  8.0 260.8 %reduce-scatter.3.cloned.1.call-start = ((), (), s32[]{:S(2)}) async-start(), calls=%async_computation.7 | async-start | bytes 23592960 | tf_op jit(solution)/shard_map/reduce_scatter | solution.py:106
  26.2 0.7 copy-start.3
  118.5 0.9 copy-start.4
  118.5 8.3 copy-start.11
  118.5 25.6 %copy-start.10 = (s32[3]{0:T(128)S(1)}, s32[3]{0:T(128)}, u32[]{:S(2)}) copy-start(s32[3]{0:T(128)} %param.22) | copy-start | bytes 40
  118.5 25.7 %copy-start.9 = (s32[3,4]{1,0:T(4,128)S(1)}, s32[3,4]{1,0:T(4,128)}, u32[]{:S(2)}) copy-start(s32[3,4]{1,0:T(4,128)} %param.21) | copy-start | bytes 148
  119.4 24.9 %copy-start.6 = (f32[4,1536]{1,0:T(4,128)S(1)}, f32[4,1536]{1,0:T(4,128)}, u32[]{:S(2)}) copy-start(f32[4,1536]{1,0:T(4,128)} %param.17) | copy-start | bytes 73732
  119.4 25.0 %copy-start.5 = (bf16[3,3,1536]{2,1,0:T(4,128)(2,1)S(1)}, bf16[3,3,1536]{2,1,0:T(4,128)(2,1)}, u32[]{:S(2)}) copy-start(bf16[3,3,1536]{2,1,0:T(4,128)(2,1)} %param.18) | copy-start | bytes 82948
  120.4 28.5 %all-to-all-start.1 = ((bf16[32,2,512]{2,1,0:T(2,128)(2,1)}), bf16[32,2,512]{2,1,0:T(2,128)(2,1)S(1)}, u32[]{:S(2)}, u32[]{:S(2)}) async-start(bf16[32,2,512]{2,1,0:T(2,128)(2,1)} %reshape.350), calls=%async_computation.1 | async-start | bytes 131072 | tf_op jit(solution)/shard_map/all_to_all | solution.py:95
  126.7 752.4 %all-gather.2.cloned.1.call-start = ((), (), s32[]{:S(2)}) async-start(), calls=%async_computation.8 | async-start | bytes 2162688 | tf_op jit(solution)/shard_map/all_gather | solution.py:102
  149.8 966.9 %reduce-scatter.5.cloned.1.call-start = ((), (), s32[]{:S(2)}) async-start(), calls=%async_computation.9 | async-start | bytes 7864320 | tf_op jit(solution)/shard_map/reduce_scatter | solution.py:158
  308.6 3.8 copy-start.2
  869.7 3.4 copy-start.8
  887.3 0.7 copy-start.7
  889.8 54.0 %all-to-all-start.3 = ((s32[32,1,1]{2,1,0:T(1,128)}), s32[32,1,1]{2,1,0:T(1,128)S(1)}, u32[]{:S(2)}, u32[]{:S(2)}) async-start(s32[32,1,1]{2,1,0:T(1,128)} %copy.145), calls=%async_computation.5 | async-start | bytes 32768 | tf_op jit(solution)/shard_map/all_to_all | solution.py:194
  943.7 146.4 %all-to-all-start.4 = ((bf16[32,128,2,512]{3,1,2,0:T(8,128)(2,1)}), bf16[32,128,2,512]{3,1,2,0:T(8,128)(2,1)}, u32[]{:S(2)}, u32[]{:S(2)}) async-start(bf16[32,128,2,512]{3,1,2,0:T(8,128)(2,1)} %scatter_fusion), calls=%async_computation.6 | async-start | bytes 16777216 | tf_op jit(solution)/shard_map/all_to_all | solution.py:193
  1092.2 24.5 %copy-start.1 = (bf16[1536,512]{1,0:T(8,128)(2,1)S(1)}, bf16[1536,512]{1,0:T(8,128)(2,1)}, u32[]{:S(2)}) copy-start(bf16[1536,512]{1,0:T(8,128)(2,1)} %param.13) | copy-start | bytes 4718596
Sparse Core Ops, SparseCore 0:
  118.6 150.0 reduce-scatter.2
  887.4 64.4 reduce-scatter.4
Sparse Core Ops, SparseCore 1:
  149.9 221.0 all-gather.1
